TPU v7x, 32 devices: a whole 2x2x4 slice. The times are simulated.
32 devices in a mesh: fsdp: 8 (over y, x, core), dp: 4 (over z).
Axes of the slice: x: 2, y: 2, z: 4, core: 2. Of those that a mesh axis runs over, the one named last changes fastest.
Arguments:
- hidden: bfloat16 [8192, 14336], P(('fsdp', 'dp')), may hold values from -6 to 6
- cotangent: bfloat16 [8192, 4096], P(('fsdp', 'dp')), may hold values from -6 to 6
- tiles: bfloat16 [64, 128, 128], P('fsdp'), may hold values from -0.25 to 0.25
- tile_rows: int32 [64], P('fsdp'), may hold values from 0 to 111, as said below
- tile_cols: int32 [64], P('fsdp'), may hold values from 0 to 31, as said below
- counts: int32 [8], P('fsdp'), may hold values from 1 to 8, as said below
Outputs:
- layer_out: bfloat16 [8192, 4096], P(('fsdp', 'dp'))
- hidden_grad: bfloat16 [8192, 14336], P(('fsdp', 'dp'))
- weight_grad: float32 [64, 128, 128], P('fsdp')
Inputs may be any that keep to these rules, and one draw needn't show every extreme that they name: `tile_rows`: every slot (live or not) names a different block; the row block is below 112. `tile_cols`: the column block is below 32. `counts`: some owner has all 8 slots live in every draw.
All inputs are finite; a program needn't handle non-finite values.
Results may differ from a plain program's by a relative error of at most 0.0085.
Values may be sent and summed in bfloat16 or wider, within the bound.
A program may use at most 192 MiB of HBM per device.

v0:
```python
import math
import jax
import jax.numpy as jnp
from jax import lax
from jax.sharding import PartitionSpec as P


def one_hot_of(ids, width):
    return (ids[:, None] == jnp.arange(width, dtype=jnp.int32)[None, :]).astype(jnp.bfloat16)


def select_blocks(blocks, ids):
    table = one_hot_of(ids, blocks.shape[1])
    chosen = jnp.einsum("tbe,kb->tke", blocks, table, preferred_element_type=jnp.float32)
    return chosen.astype(jnp.bfloat16)


def place_blocks(partial_value, ids, width):
    table = one_hot_of(ids, width).astype(jnp.float32)
    return jnp.einsum("tke,kb->tbe", partial_value, table)


def shards(hidden, cotangent, tiles, tile_rows, tile_cols, counts):
    tokens = hidden.shape[0]
    slots_own = tiles.shape[0]
    edge_len = tiles.shape[1]
    blocks_ff = hidden.shape[1] // edge_len
    blocks_model = cotangent.shape[1] // edge_len
    live_slots = jnp.arange(slots_own) < counts[0]
    masked = jnp.where(live_slots[:, None, None], tiles, jnp.zeros_like(tiles))
    all_rows, all_cols = (
        lax.all_gather(tile_rows, "fsdp", axis=0, tiled=True),
        lax.all_gather(tile_cols, "fsdp", axis=0, tiled=True),
    )
    hidden_blocks = hidden.reshape(tokens, blocks_ff, edge_len)
    upstream_blocks = cotangent.reshape(tokens, blocks_model, edge_len)
    gathered = lax.all_gather(masked, "fsdp", axis=0, tiled=True)
    row_ids = all_rows
    col_ids = all_cols
    picked = select_blocks(hidden_blocks, row_ids)
    partial_value = jnp.einsum("tkf,kfd->tkd", picked, gathered, preferred_element_type=jnp.float32)
    layer_acc = place_blocks(partial_value, col_ids, blocks_model)
    row_ids = all_rows
    col_ids = all_cols
    upstream = select_blocks(upstream_blocks, col_ids)
    partial_value = jnp.einsum(
        "tkd,kfd->tkf", upstream, gathered, preferred_element_type=jnp.float32
    )
    grad_acc = place_blocks(partial_value, row_ids, blocks_ff)
    row_ids = all_rows
    col_ids = all_cols
    picked = select_blocks(hidden_blocks, row_ids)
    upstream = select_blocks(upstream_blocks, col_ids)
    owned = lax.psum_scatter(
        jnp.einsum("tkf,tkd->kfd", picked, upstream, preferred_element_type=jnp.float32),
        "fsdp",
        scatter_dimension=0,
        tiled=True,
    )
    summed = lax.psum(owned, "dp")
    raw_grad = jnp.where(live_slots[:, None, None], summed, jnp.zeros_like(summed))
    local_squares = jnp.sum(raw_grad * raw_grad)
    local_entries = counts[0].astype(jnp.float32) * edge_len * edge_len
    squares, entries = lax.psum((local_squares, local_entries), "fsdp")
    spread = jnp.sqrt(squares / entries)
    root_tokens = math.sqrt(tokens * lax.axis_size("fsdp") * lax.axis_size("dp"))
    factor = jnp.minimum(1.0, 0.5 * root_tokens / spread) / root_tokens
    layer_out = layer_acc.reshape(tokens, blocks_model * edge_len).astype(jnp.bfloat16)
    hidden_grad = grad_acc.reshape(tokens, blocks_ff * edge_len).astype(jnp.bfloat16)
    return (layer_out, hidden_grad, raw_grad * factor)


def solution(mesh):
    placed = (
        P(("fsdp", "dp"), None),
        P(("fsdp", "dp"), None),
        P("fsdp", None, None),
        P("fsdp"),
        P("fsdp"),
        P("fsdp"),
    )
    return jax.shard_map(
        shards,
        mesh=mesh,
        in_specs=placed,
        out_specs=(P(("fsdp", "dp"), None), P(("fsdp", "dp"), None), P("fsdp", None, None)),
        check_vma=False,
    )
```

profile of v0, /device:TPU:0, one launch (start us, length us, event | category | flops | bytes accessed | tf_op | source)
XLA Modules:
  0.0 171.5 jit_solution(11835242717945344327)
XLA Ops:
  7.2 0.0 all-gather.2.cloned.1.call-start
  7.9 1.7 %broadcast_select_fusion = bf16[8,128,128]{2,1,0:T(8,128)(2,1)} fusion(bf16[8,128,128]{2,1,0:T(8,128)(2,1)} %param.8, pred[8]{0:T(512)(128)(4,1)S(1)} %iota_compare_fusion.2), kind=kLoop, calls=%fused_computation.16 | loop fusion | flops 131072 | bytes 524296 | tf_op jit(solution)/shard_map/jit(_where)/select_n | solution.py:30
  9.6 0.0 all-gather.2.cloned.1.call-update
  9.6 0.0 reduce-scatter.2.cloned.1.call-start
  9.7 0.0 copy-start.8
  9.7 0.0 copy-start.6
  9.7 0.0 copy-start.7
  9.7 7.8 %copy.16 = bf16[32,8,112,128]{3,2,1,0:T(8,128)(2,1)} copy(bf16[32,8,112,128]{3,1,2,0:T(8,128)(2,1)} %bitcast.50) | data formatting | bytes 14680064
  17.6 0.0 copy-done.8
  17.6 0.6 dynamic-slice
  18.7 0.0 copy-done.6
  18.7 0.2 dynamic-update-slice
  19.0 0.0 copy-done.7
  19.0 0.2 dynamic-update-slice.1
  19.2 9.7 %all-reduce.2 = (s32[64]{0:T(128)S(1)}, s32[64]{0:T(128)S(1)}) all-reduce(s32[64]{0:T(128)S(1)} %dynamic-update-slice.1, s32[64]{0:T(128)S(1)} %dynamic-update-slice), channel_id=1, replica_groups=mesh['fsdp'=8,'dp'=4] {'fsdp'}, use_global_device_ids=true, to_apply=%add.1 | all-reduce | flops 128 | bytes 1024
  28.9 6.4 %convert_bitcast_fusion.1 = bf16[256,64,128]{2,1,0:T(8,128)(2,1)} fusion(bf16[256,112,128]{2,1,0:T(8,128)(2,1)} %bitcast.46, s32[64]{0:T(128)S(1)} %get-tuple-element.3), kind=kOutput, calls=%fused_computation.7 | convolution fusion | flops 471866368 | bytes 11534592 | tf_op jit(solution)/shard_map/tbe,kb->tke/dot_general | solution.py:14
  35.3 0.0 copy-start.5
  35.3 7.1 %copy.11 = bf16[256,64,128]{0,2,1:T(8,128)(2,1)} copy(bf16[256,64,128]{2,1,0:T(8,128)(2,1)} %convert_bitcast_fusion.1) | data formatting | bytes 8388608 | tf_op jit(solution)/shard_map/convert_element_type | solution.py:15
  42.3 0.0 copy-done.5
  42.3 0.5 copy.18
  42.8 0.0 copy-start
  42.8 1.3 convert_bitcast_fusion
  44.1 0.0 copy-start.1
  44.1 2.0 %copy-done.1 = bf16[256,64,128]{2,1,0:T(8,128)(2,1)} copy-done((bf16[256,64,128]{2,1,0:T(8,128)(2,1)}, bf16[256,64,128]{2,1,0:T(8,128)(2,1)S(1)}, u32[]{:S(2)}) %copy-start.1) | copy-done | bytes 4194328
  46.1 0.0 copy-done
  46.1 7.2 %fusion.9 = f32[64,128,128]{2,1,0:T(8,128)} fusion(bf16[256,64,128]{0,2,1:T(8,128)(2,1)S(1)} %copy-done, bf16[256,64,128]{2,1,0:T(8,128)(2,1)S(1)} %convert_bitcast_fusion), kind=kOutput, calls=%fused_computation.10 | convolution fusion | flops 536870912 | bytes 12582912 | tf_op jit(solution)/shard_map/tkf,tkd->kfd/dot_general | solution.py:55
  53.3 0.0 reduce-scatter.2.cloned.1.call-update
  53.4 0.2 all-reduce.6.cloned.1.call-start
  53.6 0.0 all-gather.2.cloned.1.call-done
  53.6 9.4 %fusion.7 = bf16[64,128,256]{2,1,0:T(8,128)(2,1)} fusion(bf16[64,128,128]{2,1,0:T(8,128)(2,1)} %all-gather.2.cloned.1.call-done, bf16[256,64,128]{2,1,0:T(8,128)(2,1)} %copy-done.1), kind=kOutput, calls=%fused_computation.8 | convolution fusion | flops 536870912 | bytes 10485760 | tf_op jit(solution)/shard_map/tkd,kfd->tkf/dot_general | solution.py:46
  63.0 6.6 %copy.15 = bf16[64,128,256]{1,0,2:T(8,128)(2,1)} copy(bf16[64,128,256]{2,1,0:T(8,128)(2,1)} %fusion.7) | data formatting | bytes 8388608 | tf_op jit(solution)/shard_map/tkd,kfd->tkf/dot_general | solution.py:46
  69.7 0.0 copy-start.3
  69.7 7.6 %fusion.4 = bf16[112,256,128]{2,0,1:T(8,128)(2,1)} fusion(bf16[64,128,256]{1,0,2:T(8,128)(2,1)} %copy.15, s32[64]{0:T(128)S(1)} %get-tuple-element.3), kind=kOutput, calls=%fused_computation.5 | convolution fusion | flops 469769216 | bytes 11534592 | tf_op jit(solution)/shard_map/tke,kb->tbe/dot_general | solution.py:20
  77.3 26.8 %reduce-scatter.2.cloned.1.call-done = f32[8,128,128]{2,1,0:T(8,128)} async-done(((f32[64,128,128]{2,1,0:T(8,128)}), f32[8,128,128]{2,1,0:T(8,128)}) %reduce-scatter.2.cloned.1.call-update) | async-done | bytes 524304 | tf_op jit(solution)/shard_map/reduce_scatter | solution.py:54
  104.1 0.0 all-reduce.6.cloned.1.call-update
  104.1 0.0 copy-done.3
  104.1 0.0 copy-start.2
  104.1 5.6 %fusion.24 = bf16[64,128,256]{2,1,0:T(8,128)(2,1)} fusion(bf16[64,128,128]{2,1,0:T(8,128)(2,1)S(1)} %copy-done.3, bf16[256,64,128]{0,2,1:T(8,128)(2,1)} %copy.11), kind=kOutput, calls=%fused_computation.26 | convolution fusion | flops 536870912 | bytes 10485760 | tf_op jit(solution)/shard_map/tkf,kfd->tkd/dot_general | solution.py:41
  109.8 0.0 copy-done.2
  109.8 4.9 %copy.26 = bf16[32,8,112,128]{3,1,2,0:T(8,128)(2,1)} copy(bf16[32,8,112,128]{3,2,1,0:T(8,128)(2,1)S(1)} %bitcast.47) | data formatting | bytes 14680064
  114.7 6.5 %copy.13 = bf16[64,128,256]{1,0,2:T(8,128)(2,1)} copy(bf16[64,128,256]{2,1,0:T(8,128)(2,1)} %fusion.24) | data formatting | bytes 8388608 | tf_op jit(solution)/shard_map/tkf,kfd->tkd/dot_general | solution.py:41
  121.2 2.9 %fusion.11 = bf16[32,256,128]{2,0,1:T(8,128)(2,1)S(1)} fusion(bf16[64,128,256]{1,0,2:T(8,128)(2,1)} %copy.13, s32[64]{0:T(128)S(1)} %get-tuple-element.4), kind=kOutput, calls=%fused_computation.13 | convolution fusion | flops 134219776 | bytes 6291712 | tf_op jit(solution)/shard_map/tke,kb->tbe/dot_general | solution.py:20
  124.1 21.0 %all-reduce.6.cloned.1.call-done = f32[8,128,128]{2,1,0:T(8,128)} async-done(((f32[8,128,128]{2,1,0:T(8,128)}), f32[8,128,128]{2,1,0:T(8,128)}) %all-reduce.6.cloned.1.call-update) | async-done | bytes 524304 | tf_op jit(solution)/shard_map/psum | solution.py:60
  145.2 0.0 copy-start.4
  145.2 1.9 %multiply_reduce_fusion = f32[]{:T(128)} fusion(f32[8,128,128]{2,1,0:T(8,128)} %all-reduce.6.cloned.1.call-done, pred[8]{0:T(512)(128)(4,1)S(1)} %iota_compare_fusion.2), kind=kLoop, calls=%fused_computation.14 | loop fusion | flops 393215 | bytes 524300 | tf_op jit(solution)/shard_map/reduce_sum | solution.py:62
  147.1 2.3 %copy.27 = bf16[32,8,32,128]{3,1,2,0:T(8,128)(2,1)} copy(bf16[32,8,32,128]{3,2,1,0:T(8,128)(2,1)S(1)} %bitcast.48) | data formatting | bytes 4194304
  149.4 13.3 %all-reduce.3 = (f32[]{:T(128)}, f32[]{:T(128)}) all-reduce(f32[]{:T(128)} %multiply_reduce_fusion, f32[]{:T(128)S(6)} %mul.14), channel_id=1, replica_groups=mesh['fsdp'=8,'dp'=4] {'fsdp'}, use_global_device_ids=true, to_apply=%region_3.4 | all-reduce | flops 2 | bytes 16 | tf_op jit(solution)/shard_map/psum | solution.py:64
  164.0 0.0 copy-done.4
  164.0 0.9 select_multiply_fusion
  (3 shorter events, 0.0 us)
Async XLA Ops:
  7.2 46.5 %all-gather.2.cloned.1.call-start = ((), (), s32[]{:S(2)}) async-start(), calls=%async_computation.1 | async-start | bytes 2359296 | tf_op jit(solution)/shard_map/all_gather | solution.py:37
  9.6 94.5 %reduce-scatter.2.cloned.1.call-start = ((), (), s32[]{:S(2)}) async-start(), calls=%async_computation.2 | async-start | bytes 4718592 | tf_op jit(solution)/shard_map/reduce_scatter | solution.py:54
  9.7 7.9 %copy-start.8 = (u32[32]{0:T(128)S(1)}, u32[32]{0:T(128)}, u32[]{:S(2)}) copy-start(u32[32]{0:T(128)} %constant.18) | copy-start | bytes 388
  9.7 9.0 %copy-start.6 = (s32[8]{0:T(128)S(1)}, s32[8]{0:T(128)}, u32[]{:S(2)}) copy-start(s32[8]{0:T(128)} %param.10) | copy-start | bytes 100
  9.7 9.3 %copy-start.7 = (s32[8]{0:T(128)S(1)}, s32[8]{0:T(128)}, u32[]{:S(2)}) copy-start(s32[8]{0:T(128)} %param.9) | copy-start | bytes 100
  35.3 7.1 %copy-start.5 = (bf16[256,4096]{1,0:T(8,128)(2,1)S(1)}, bf16[256,4096]{1,0:T(8,128)(2,1)}, u32[]{:S(2)}) copy-start(bf16[256,4096]{1,0:T(8,128)(2,1)} %param.7) | copy-start | bytes 6291460
  42.8 3.3 %copy-start = (bf16[256,64,128]{0,2,1:T(8,128)(2,1)S(1)}, bf16[256,64,128]{0,2,1:T(8,128)(2,1)}, u32[]{:S(2)}) copy-start(bf16[256,64,128]{0,2,1:T(8,128)(2,1)} %copy.11) | copy-start | bytes 12582916
  44.1 2.0 %copy-start.1 = (bf16[256,64,128]{2,1,0:T(8,128)(2,1)}, bf16[256,64,128]{2,1,0:T(8,128)(2,1)S(1)}, u32[]{:S(2)}) copy-start(bf16[256,64,128]{2,1,0:T(8,128)(2,1)S(1)} %convert_bitcast_fusion) | copy-start | bytes 12582916
  53.4 91.8 %all-reduce.6.cloned.1.call-start = ((), (), s32[]{:S(2)}) async-start(), calls=%async_computation.3 | async-start | bytes 1048576 | tf_op jit(solution)/shard_map/psum | solution.py:60
  69.7 34.5 %copy-start.3 = (bf16[64,128,128]{2,1,0:T(8,128)(2,1)S(1)}, bf16[64,128,128]{2,1,0:T(8,128)(2,1)}, u32[]{:S(2)}) copy-start(bf16[64,128,128]{2,1,0:T(8,128)(2,1)} %all-gather.2.cloned.1.call-done) | copy-start | bytes 6291460
  104.1 5.6 %copy-start.2 = (bf16[112,256,128]{2,0,1:T(8,128)(2,1)S(1)}, bf16[112,256,128]{2,0,1:T(8,128)(2,1)}, u32[]{:S(2)}) copy-start(bf16[112,256,128]{2,0,1:T(8,128)(2,1)} %fusion.4) | copy-start | bytes 22020100
  145.2 18.9 %copy-start.4 = (f32[8,128,128]{2,1,0:T(8,128)S(1)}, f32[8,128,128]{2,1,0:T(8,128)}, u32[]{:S(2)}) copy-start(f32[8,128,128]{2,1,0:T(8,128)} %all-reduce.6.cloned.1.call-done) | copy-start | bytes 1572868
Sparse Core Ops, SparseCore 0:
  10.4 30.5 all-gather.1
  53.5 50.5 reduce-scatter.1
  106.4 38.6 all-reduce.5
where the time goes:
time: 172 us; the launch traced here: 171 us
  waiting for transfers between devices  47.9 us (28%)
  matrix products  40.4 us (23%)
  local copies, waits for them, and re-layouts  38.9 us (23%)
  blocking collectives  23 us (13%)
  between operations  16.4 us (10%)
  other arithmetic  4.57 us (3%)
    reduce_scatter x1, waiting for transfers between devices, shards(): lax.psum_scatter(jnp.einsum('tkf,tkd->kfd', picked, upstream, preferred_e...  26.8 us
    psum x1, waiting for transfers between devices, shards(): summed = lax.psum(owned, 'dp')  21 us
    unnamed x27, local copies, waits for them, and re-layouts  18.6 us
    psum x1, blocking collectives, shards(): squares, entries = lax.psum((local_squares, local_entries), 'fsdp')  13.3 us
    dot_general x2, matrix products, place_blocks(): return jnp.einsum('tke,kb->tbe', partial_value, table)  10.5 us
    unnamed x1, blocking collectives  9.69 us
    dot_general x1, matrix products, shards(): jnp.einsum('tkd,kfd->tkf', upstream, gathered, preferred_element_type=jnp...  9.41 us
    dot_general x2, matrix products, select_blocks(): jnp.einsum('tbe,kb->tke', blocks, table, preferred_element_type=jnp.float32)  7.66 us
  transfers between devices with their start and end apart: 3, of which 2 were waited for; matrix products, arithmetic and copies ran while one was open for 44% of the time, Pallas kernels for 0%

commit v1 on v0

--- a/solution.py
+++ b/solution.py
@@ -57,7 +57,9 @@
         scatter_dimension=0,
         tiled=True,
     )
-    summed = lax.psum(owned, "dp")
+    summed = owned
+    for hop in (1, 2):
+        summed = summed + lax.ppermute(summed, "dp", [(dev, dev ^ hop) for dev in range(4)])
     raw_grad = jnp.where(live_slots[:, None, None], summed, jnp.zeros_like(summed))
     local_squares = jnp.sum(raw_grad * raw_grad)
     local_entries = counts[0].astype(jnp.float32) * edge_len * edge_len

time: 172 us -> 205 us (1.19)
  waiting for transfers between devices: 47.9 us -> 84.2 us
  matrix products: 40.4 us -> 34.9 us
  starting transfers between devices: 0.3 us -> 4.22 us
    all_gather x1, waiting for transfers between devices: 0.02 us -> 28.8 us  [shards(): gathered = lax.all_gather(masked, 'fsdp', axis=0, tiled=True)]
    reduce_scatter x1, waiting for transfers between devices: 26.8 us -> 49.2 us  [shards(): lax.psum_scatter(jnp.einsum('tkf,tkd->kfd', picked, upstream, preferred_e...]
    psum x1 -> x0, waiting for transfers between devices: 21 us -> none  [shards(): summed = lax.psum(owned, 'dp')]
    ppermute x0 -> x2, waiting for transfers between devices: none -> 6.17 us  [shards(): lax.ppermute(summed, 'dp', [(dev, dev ^ hop) for dev in range(4)])]
    ppermute x0 -> x2, starting transfers between devices: none -> 3.96 us  [shards(): lax.ppermute(summed, 'dp', [(dev, dev ^ hop) for dev in range(4)])]
    dot_general x2, matrix products: 10.5 us -> 7.38 us  [place_blocks(): return jnp.einsum('tke,kb->tbe', partial_value, table)]
    dot_general x1, matrix products: 5.61 us -> 3.24 us  [shards(): jnp.einsum('tkf,kfd->tkd', picked, gathered, preferred_element_type=jnp.f...]
    unnamed x27 -> x29, local copies, waits for them, and re-layouts: 18.6 us -> 18.6 us
  transfers between devices with their start and end apart: 3 -> 4, of which waited for: 2 -> 3; matrix products, arithmetic and copies ran while one was open for 44% -> 19% of each run, Pallas kernels for 0% -> 0%
where the time goes in v1:
time: 205 us; the launch traced here: 204 us
  waiting for transfers between devices  84.2 us (41%)
  local copies, waits for them, and re-layouts  38.7 us (19%)
  matrix products  34.9 us (17%)
  blocking collectives  22.4 us (11%)
  between operations  16.9 us (8%)
  starting transfers between devices  4.22 us (2%)
  other arithmetic  2.57 us (1%)
    reduce_scatter x1, waiting for transfers between devices, shards(): lax.psum_scatter(jnp.einsum('tkf,tkd->kfd', picked, upstream, preferred_e...  49.2 us
    all_gather x1, waiting for transfers between devices, shards(): gathered = lax.all_gather(masked, 'fsdp', axis=0, tiled=True)  28.8 us
    unnamed x29, local copies, waits for them, and re-layouts  18.6 us
    psum x1, blocking collectives, shards(): squares, entries = lax.psum((local_squares, local_entries), 'fsdp')  12.9 us
    unnamed x1, blocking collectives  9.49 us
    dot_general x1, matrix products, shards(): jnp.einsum('tkd,kfd->tkf', upstream, gathered, preferred_element_type=jnp...  9.43 us
    dot_general x2, matrix products, select_blocks(): jnp.einsum('tbe,kb->tke', blocks, table, preferred_element_type=jnp.float32)  7.61 us
    dot_general x2, matrix products, place_blocks(): return jnp.einsum('tke,kb->tbe', partial_value, table)  7.38 us
  transfers between devices with their start and end apart: 4, of which 3 were waited for; matrix products, arithmetic and copies ran while one was open for 19% of the time, Pallas kernels for 0%

profile of v1, /device:TPU:0, one launch (start us, length us, event | category | flops | bytes accessed | tf_op | source)
XLA Modules:
  0.0 203.9 jit_solution(4988000121350219583)
XLA Ops:
  7.2 0.0 reduce-scatter.2.cloned.1.call-start
  7.2 0.0 copy-start.9
  7.2 0.0 copy-start.7
  7.2 0.0 copy-start.8
  7.3 7.8 %copy.16 = bf16[32,8,112,128]{3,2,1,0:T(8,128)(2,1)} copy(bf16[32,8,112,128]{3,1,2,0:T(8,128)(2,1)} %bitcast.50) | data formatting | bytes 14680064
  15.1 0.0 copy-done.9
  15.1 0.6 dynamic-slice
  16.3 0.0 copy-done.7
  16.4 0.2 dynamic-update-slice
  16.6 0.0 copy-done.8
  16.6 0.2 dynamic-update-slice.1
  16.8 9.5 %all-reduce.2 = (s32[64]{0:T(128)S(1)}, s32[64]{0:T(128)S(1)}) all-reduce(s32[64]{0:T(128)S(1)} %dynamic-update-slice.1, s32[64]{0:T(128)S(1)} %dynamic-update-slice), channel_id=1, replica_groups=mesh['fsdp'=8,'dp'=4] {'fsdp'}, use_global_device_ids=true, to_apply=%add.1 | all-reduce | flops 128 | bytes 1024
  26.3 6.3 %convert_bitcast_fusion.1 = bf16[256,64,128]{2,1,0:T(8,128)(2,1)} fusion(bf16[256,112,128]{2,1,0:T(8,128)(2,1)} %bitcast.46, s32[64]{0:T(128)S(1)} %get-tuple-element.3), kind=kOutput, calls=%fused_computation.7 | convolution fusion | flops 471866368 | bytes 11534592 | tf_op jit(solution)/shard_map/tbe,kb->tke/dot_general | solution.py:14
  32.6 0.0 copy-start.4
  32.6 7.0 %copy.11 = bf16[256,64,128]{0,2,1:T(8,128)(2,1)} copy(bf16[256,64,128]{2,1,0:T(8,128)(2,1)} %convert_bitcast_fusion.1) | data formatting | bytes 8388608 | tf_op jit(solution)/shard_map/convert_element_type | solution.py:15
  39.6 0.0 copy-done.4
  39.6 0.5 copy.18
  40.1 0.0 copy-start
  40.1 1.3 convert_bitcast_fusion
  41.4 0.0 copy-start.2
  41.4 1.9 copy-done.2
  43.3 0.0 copy-done
  43.3 7.2 %fusion.9 = f32[64,128,128]{2,1,0:T(8,128)} fusion(bf16[256,64,128]{0,2,1:T(8,128)(2,1)S(1)} %copy-done, bf16[256,64,128]{2,1,0:T(8,128)(2,1)S(1)} %convert_bitcast_fusion), kind=kOutput, calls=%fused_computation.10 | convolution fusion | flops 536870912 | bytes 12582912 | tf_op jit(solution)/shard_map/tkf,tkd->kfd/dot_general | solution.py:55
  50.5 0.0 copy-start.6
  50.5 0.0 reduce-scatter.2.cloned.1.call-update
  50.6 0.2 all-gather.2.cloned.1.call-start
  51.5 0.0 copy-done.6
  51.5 0.8 broadcast_select_fusion
  52.3 0.0 all-gather.2.cloned.1.call-update
  52.3 49.2 %reduce-scatter.2.cloned.1.call-done = f32[8,128,128]{2,1,0:T(8,128)} async-done(((f32[64,128,128]{2,1,0:T(8,128)}), f32[8,128,128]{2,1,0:T(8,128)}) %reduce-scatter.2.cloned.1.call-update) | async-done | bytes 524304 | tf_op jit(solution)/shard_map/reduce_scatter | solution.py:54
  101.6 1.5 collective-permute-start
  103.1 28.8 %all-gather.2.cloned.1.call-done = bf16[64,128,128]{2,1,0:T(8,128)(2,1)} async-done(((bf16[8,128,128]{2,1,0:T(8,128)(2,1)}), bf16[64,128,128]{2,1,0:T(8,128)(2,1)}) %all-gather.2.cloned.1.call-update) | async-done | bytes 2097168 | tf_op jit(solution)/shard_map/all_gather | solution.py:37
  131.8 9.4 %fusion.7 = bf16[64,128,256]{2,1,0:T(8,128)(2,1)} fusion(bf16[64,128,128]{2,1,0:T(8,128)(2,1)} %all-gather.2.cloned.1.call-done, bf16[256,64,128]{2,1,0:T(8,128)(2,1)} %copy-done.2), kind=kOutput, calls=%fused_computation.8 | convolution fusion | flops 536870912 | bytes 10485760 | tf_op jit(solution)/shard_map/tkd,kfd->tkf/dot_general | solution.py:46
  141.3 6.6 %copy.15 = bf16[64,128,256]{1,0,2:T(8,128)(2,1)} copy(bf16[64,128,256]{2,1,0:T(8,128)(2,1)} %fusion.7) | data formatting | bytes 8388608 | tf_op jit(solution)/shard_map/tkd,kfd->tkf/dot_general | solution.py:46
  147.8 0.0 copy-start.5
  147.8 0.0 copy-start.1
  147.8 0.0 copy-start.3
  147.8 4.5 %fusion.4 = bf16[112,256,128]{2,0,1:T(8,128)(2,1)S(1)} fusion(bf16[64,128,256]{1,0,2:T(8,128)(2,1)} %copy.15, s32[64]{0:T(128)S(1)} %get-tuple-element.3), kind=kOutput, calls=%fused_computation.5 | convolution fusion | flops 469769216 | bytes 11534592 | tf_op jit(solution)/shard_map/tke,kb->tbe/dot_general | solution.py:20
  152.3 0.0 collective-permute-done
  152.4 0.0 copy-done.5
  152.4 0.1 add.12
  152.4 2.5 %collective-permute-start.1 = (f32[8,128,128]{2,1,0:T(8,128)S(1)}, f32[8,128,128]{2,1,0:T(8,128)S(1)}, u32[]{:S(2)}, u32[]{:S(2)}) collective-permute-start(f32[8,128,128]{2,1,0:T(8,128)S(1)} %add.12), channel_id=1, source_target_pairs={{0,2},{1,3},{2,0},{3,1},{4,6},{5,7},{6,4},{7,5},{8,10},{9,11},{10,... | collective-permute-start | bytes 1572872 | tf_op jit(solution)/shard_map/ppermute | solution.py:62
  154.9 0.0 copy-done.1
  154.9 0.0 copy-done.3
  154.9 3.2 %fusion.24 = bf16[64,128,256]{2,1,0:T(8,128)(2,1)} fusion(bf16[64,128,128]{2,1,0:T(8,128)(2,1)S(1)} %copy-done.3, bf16[256,64,128]{0,2,1:T(8,128)(2,1)S(1)} %copy-done.1), kind=kOutput, calls=%fused_computation.27 | convolution fusion | flops 536870912 | bytes 10485760 | tf_op jit(solution)/shard_map/tkf,kfd->tkd/dot_general | solution.py:41
  158.1 4.9 %copy.26 = bf16[32,8,112,128]{3,1,2,0:T(8,128)(2,1)} copy(bf16[32,8,112,128]{3,2,1,0:T(8,128)(2,1)S(1)} %bitcast.47) | data formatting | bytes 14680064
  163.1 6.6 %copy.13 = bf16[64,128,256]{1,0,2:T(8,128)(2,1)} copy(bf16[64,128,256]{2,1,0:T(8,128)(2,1)} %fusion.24) | data formatting | bytes 8388608 | tf_op jit(solution)/shard_map/tkf,kfd->tkd/dot_general | solution.py:41
  169.6 2.9 %fusion.11 = bf16[32,256,128]{2,0,1:T(8,128)(2,1)S(1)} fusion(bf16[64,128,256]{1,0,2:T(8,128)(2,1)} %copy.13, s32[64]{0:T(128)S(1)} %get-tuple-element.4), kind=kOutput, calls=%fused_computation.13 | convolution fusion | flops 134219776 | bytes 6291712 | tf_op jit(solution)/shard_map/tke,kb->tbe/dot_general | solution.py:20
  172.5 6.2 %collective-permute-done.1 = f32[8,128,128]{2,1,0:T(8,128)S(1)} collective-permute-done((f32[8,128,128]{2,1,0:T(8,128)S(1)}, f32[8,128,128]{2,1,0:T(8,128)S(1)}, u32[]{:S(2)}, u32[]{:S(2)}) %collective-permute-start.1) | collective-permute-done | bytes 524320 | tf_op jit(solution)/shard_map/ppermute | solution.py:62
  178.7 0.8 multiply_reduce_fusion
  179.5 2.3 %copy.27 = bf16[32,8,32,128]{3,1,2,0:T(8,128)(2,1)} copy(bf16[32,8,32,128]{3,2,1,0:T(8,128)(2,1)S(1)} %bitcast.48) | data formatting | bytes 4194304
  181.8 12.9 %all-reduce.3 = (f32[]{:T(128)}, f32[]{:T(128)}) all-reduce(f32[]{:T(128)} %multiply_reduce_fusion, f32[]{:T(128)S(6)} %mul.14), channel_id=1, replica_groups=mesh['fsdp'=8,'dp'=4] {'fsdp'}, use_global_device_ids=true, to_apply=%region_2.3 | all-reduce | flops 2 | bytes 16 | tf_op jit(solution)/shard_map/psum | solution.py:66
  196.1 0.9 broadcast_multiply_fusion
  (3 shorter events, 0.0 us)
Async XLA Ops:
  7.2 94.4 %reduce-scatter.2.cloned.1.call-start = ((), (), s32[]{:S(2)}) async-start(), calls=%async_computation.2 | async-start | bytes 4718592 | tf_op jit(solution)/shard_map/reduce_scatter | solution.py:54
  7.2 7.9 %copy-start.9 = (u32[32]{0:T(128)S(1)}, u32[32]{0:T(128)}, u32[]{:S(2)}) copy-start(u32[32]{0:T(128)} %constant.18) | copy-start | bytes 388
  7.2 9.1 %copy-start.7 = (s32[8]{0:T(128)S(1)}, s32[8]{0:T(128)}, u32[]{:S(2)}) copy-start(s32[8]{0:T(128)} %param.10) | copy-start | bytes 100
  7.2 9.4 %copy-start.8 = (s32[8]{0:T(128)S(1)}, s32[8]{0:T(128)}, u32[]{:S(2)}) copy-start(s32[8]{0:T(128)} %param.9) | copy-start | bytes 100
  32.6 7.0 %copy-start.4 = (bf16[256,4096]{1,0:T(8,128)(2,1)S(1)}, bf16[256,4096]{1,0:T(8,128)(2,1)}, u32[]{:S(2)}) copy-start(bf16[256,4096]{1,0:T(8,128)(2,1)} %param.7) | copy-start | bytes 6291460
  40.1 3.3 %copy-start = (bf16[256,64,128]{0,2,1:T(8,128)(2,1)S(1)}, bf16[256,64,128]{0,2,1:T(8,128)(2,1)}, u32[]{:S(2)}) copy-start(bf16[256,64,128]{0,2,1:T(8,128)(2,1)} %copy.11) | copy-start | bytes 12582916
  41.4 1.9 copy-start.2
  50.5 0.9 copy-start.6
  50.6 81.3 %all-gather.2.cloned.1.call-start = ((), (), s32[]{:S(2)}) async-start(), calls=%async_computation.1 | async-start | bytes 2359296 | tf_op jit(solution)/shard_map/all_gather | solution.py:37
  101.6 50.8 %collective-permute-start = (f32[8,128,128]{2,1,0:T(8,128)}, f32[8,128,128]{2,1,0:T(8,128)S(1)}, u32[]{:S(2)}, u32[]{:S(2)}) collective-permute-start(f32[8,128,128]{2,1,0:T(8,128)} %reduce-scatter.2.cloned.1.call-done), channel_id=1, source_target_pairs={{0,1},{1,0},{2,3},{3,2},{4,5},{5,4},{6,7},{7,6},{8,9},{9,8},{10,11... | collective-permute-start | bytes 1572872 | tf_op jit(solution)/shard_map/ppermute | solution.py:62
  147.8 4.5 %copy-start.5 = (f32[8,128,128]{2,1,0:T(8,128)S(1)}, f32[8,128,128]{2,1,0:T(8,128)}, u32[]{:S(2)}) copy-start(f32[8,128,128]{2,1,0:T(8,128)} %reduce-scatter.2.cloned.1.call-done) | copy-start | bytes 1572868
  147.8 7.1 %copy-start.1 = (bf16[256,64,128]{0,2,1:T(8,128)(2,1)S(1)}, bf16[256,64,128]{0,2,1:T(8,128)(2,1)}, u32[]{:S(2)}) copy-start(bf16[256,64,128]{0,2,1:T(8,128)(2,1)} %copy.11) | copy-start | bytes 12582916
  147.8 7.1 %copy-start.3 = (bf16[64,128,128]{2,1,0:T(8,128)(2,1)S(1)}, bf16[64,128,128]{2,1,0:T(8,128)(2,1)}, u32[]{:S(2)}) copy-start(bf16[64,128,128]{2,1,0:T(8,128)(2,1)} %all-gather.2.cloned.1.call-done) | copy-start | bytes 6291460
  152.4 26.3 %collective-permute-start.1 = (f32[8,128,128]{2,1,0:T(8,128)S(1)}, f32[8,128,128]{2,1,0:T(8,128)S(1)}, u32[]{:S(2)}, u32[]{:S(2)}) collective-permute-start(f32[8,128,128]{2,1,0:T(8,128)S(1)} %add.12), channel_id=1, source_target_pairs={{0,2},{1,3},{2,0},{3,1},{4,6},{5,7},{6,4},{7,5},{8,10},{9,11},{10,... | collective-permute-start | bytes 1572872 | tf_op jit(solution)/shard_map/ppermute | solution.py:62
Sparse Core Ops, SparseCore 0:
  50.7 50.8 reduce-scatter.1
  104.0 27.7 all-gather.1
